TPU v7x, 128 devices: a whole 4x4x4 slice. The times are simulated.
128 devices in a mesh: rep: 2 (over core), dom: 64 (over y, z, x).
Axes of the slice: x: 4, y: 4, z: 4, core: 2. Of those that a mesh axis runs over, the one named last changes fastest.
Arguments:
- features: bfloat16 [8192, 512], P('dom'), may hold values from -6 to 6
- tiles: bfloat16 [8192, 128, 128], P(('rep', 'dom')), may hold values from -0.359375 to 0.359375
- tile_dest: int32 [8192, 1], P(('rep', 'dom')), may hold values from 0 to 63; in each aligned block of 64 rows (0 to 63, 64 to 127, ...) at most 2 rows name the same one
- tile_count: int32 [8192], P(('rep', 'dom')), may hold values from 16 to 128
- weight: bfloat16 [512, 512], replicated, may hold values from -0.25 to 0.25
- bias: float32 [512], replicated, may hold values from -3 to 3
- cotangent: bfloat16 [8192, 512], P('dom'), may hold values from -6 to 6
Outputs:
- activated: bfloat16 [8192, 512], P('dom', 'rep')
- weight_grad: float32 [512, 512], P(None, 'rep')
- feature_grad: bfloat16 [8192, 512], P('dom', 'rep')
Inputs may be any that keep to these rules, and one draw needn't show every extreme that they name: `tile_dest`: among the tiles of one device no block is named more than 2 times, and some block is named exactly 2 times.
All inputs are finite; a program needn't handle non-finite values.
Results may differ from a plain program's by a relative error of at most 0.02.
Values may be sent and summed in bfloat16 or wider, within the bound.
A program may use at most 128 MiB of HBM per device.

v0:
```python
import jax
import jax.numpy as jnp
from jax import lax
from jax.sharding import PartitionSpec as P


def per_device(features, tiles, tile_dest, tile_count, weight, bias, cotangent):
    domains = lax.axis_size("dom")
    rep_index = lax.axis_index("rep")
    block = features.shape[0]
    width = features.shape[1]
    half = width // 2
    count_tiles = tiles.shape[0]
    slots = max(2, 2 * count_tiles // domains)
    dest = tile_dest[:, 0]
    scale = lax.rsqrt(tile_count.astype(jnp.float32))
    order = jnp.arange(count_tiles, dtype=jnp.int32)
    earlier = (dest[:, None] == dest[None, :]) & (order[None, :] < order[:, None])
    rank = jnp.sum(earlier.astype(jnp.int32), axis=1)
    slot_index = dest * slots + rank
    terms = (
        jnp.einsum("tij,jf->tif", tiles, features, preferred_element_type=jnp.float32)
        * scale[:, None, None]
    )
    send_buf = (
        jnp.zeros((domains * slots, block, width), jnp.bfloat16)
        .at[slot_index]
        .set(terms.astype(jnp.bfloat16))
    )
    received = lax.all_to_all(
        send_buf.reshape(domains, slots, block, width),
        "dom",
        split_axis=0,
        concat_axis=0,
        tiled=True,
    )
    partial_rows = jnp.sum(received, axis=(0, 1), dtype=jnp.float32)
    aggregated = lax.psum(partial_rows.astype(jnp.bfloat16), "rep")
    pre = jnp.dot(aggregated, weight, preferred_element_type=jnp.float32) + bias
    sig = jax.nn.sigmoid(pre)
    activated = lax.dynamic_slice_in_dim(pre * sig, rep_index * half, half, 1).astype(jnp.bfloat16)
    pre_grad = (cotangent.astype(jnp.float32) * sig * (1.0 + pre * (1.0 - sig))).astype(
        jnp.bfloat16
    )
    grad_half = lax.dynamic_slice_in_dim(pre_grad, rep_index * half, half, 1)
    weight_part = jnp.dot(aggregated.T, grad_half, preferred_element_type=jnp.float32)
    weight_grad = lax.psum(weight_part, "dom") / jnp.sqrt(jnp.float32(domains * block))
    row_grad = jnp.dot(pre_grad, weight.T, preferred_element_type=jnp.float32).astype(jnp.bfloat16)
    every_grad = lax.all_gather(row_grad, "dom", axis=0, tiled=True).reshape(domains, block, width)
    picked = every_grad[dest]
    back_terms = (
        jnp.einsum("tij,tif->tjf", tiles, picked, preferred_element_type=jnp.float32)
        * scale[:, None, None]
    )
    back_rows = jnp.sum(back_terms, axis=0)
    feature_grad = lax.psum_scatter(
        back_rows.astype(jnp.bfloat16), "rep", scatter_dimension=1, tiled=True
    )
    return (activated, weight_grad, feature_grad)


def solution(mesh):
    in_specs = (
        P("dom", None),
        P(("rep", "dom"), None, None),
        P(("rep", "dom"), None),
        P(("rep", "dom")),
        P(),
        P(),
        P("dom", None),
    )
    out_specs = (P("dom", "rep"), P(None, "rep"), P("dom", "rep"))
    return jax.shard_map(
        per_device, mesh=mesh, in_specs=in_specs, out_specs=out_specs, check_vma=False
    )
```

profile of v0, /device:TPU:0, one launch (start us, length us, event | category | flops | bytes accessed | tf_op | source)
XLA Modules:
  0.0 509.9 jit_solution(5944573904474104200)
XLA Ops:
  7.2 0.0 all-reduce.3.cloned.1.call-start
  7.2 1.0 convert_reduce_fusion
  8.2 0.7 fusion.7
  8.9 0.7 convert_rsqrt_fusion
  9.5 6.5 %multiply_convert_fusion = bf16[64,128,512]{2,1,0:T(8,128)(2,1)} fusion(bf16[64,128,128]{2,1,0:T(8,128)(2,1)S(1)} %copy-done, f32[64]{0:T(128)S(1)} %convert_rsqrt_fusion, bf16[128,512]{1,0:T(8,128)(2,1)} %param.7), kind=kOutput, calls=%fused_computation.3 | convolution fusion | flops 1082130432 | bytes 10617088 | tf_op jit(solution)/shard_map/tij,jf->tif/dot_general | solution.py:22
  16.0 5.9 %broadcast_in_dim.2 = bf16[128,128,512]{2,1,0:T(8,128)(2,1)} broadcast(bf16[]{:T(256)} %constant.12.clone.1), dimensions={} | broadcast | bytes 16777218 | tf_op jit(solution)/shard_map/broadcast_in_dim | solution.py:26
  21.9 22.1 %scatter_fusion = bf16[128,128,512]{2,1,0:T(8,128)(2,1)} fusion(bf16[128,128,512]{2,1,0:T(8,128)(2,1)} %broadcast_in_dim.2, s32[64]{0:T(128)S(1)} %get-tuple-element.12, bf16[64,128,512]{2,1,0:T(8,128)(2,1)} %multiply_convert_fusion), kind=kCustom, calls=%fused_computation.1 | custom fusion | bytes 25166080 | tf_op jit(solution)/shard_map/scatter | solution.py:28
  44.0 199.7 %all_to_all.5 = bf16[64,2,128,512]{3,2,1,0:T(8,128)(2,1)} all-to-all(bf16[64,2,128,512]{3,2,1,0:T(8,128)(2,1)} %bitcast.25), channel_id=1, replica_groups=mesh['rep'=2,'dom'=64] {'dom'}, dimensions={0} | all-to-all | bytes 33554432 | tf_op jit(solution)/shard_map/all_to_all | solution.py:30
  243.7 9.7 %reduce_sum.34 = bf16[128,512]{1,0:T(8,128)(2,1)} reduce(bf16[64,2,128,512]{3,2,1,0:T(8,128)(2,1)} %all_to_all.5, bf16[]{:T(256)} %constant.12.clone.1), dimensions={0,1}, to_apply=%region_2.0 | reduce | flops 8323072 | bytes 16908290 | tf_op jit(solution)/shard_map/reduce_sum | solution.py:37
  253.4 0.0 all-gather.2.cloned.1.call-start
  253.5 23.4 %all-reduce.3.cloned.1.call-done = bf16[128,512]{1,0:T(8,128)(2,1)} async-done(((bf16[128,512]{1,0:T(8,128)(2,1)}), bf16[128,512]{1,0:T(8,128)(2,1)}) %all-reduce.3.cloned.1.call-update) | async-done | bytes 131088 | tf_op jit(solution)/shard_map/psum | solution.py:38
  276.9 1.2 multiply_convert_fusion.1
  278.2 1.0 convolution_convert_fusion
  279.1 0.0 all-reduce.5.cloned.1.call-start
  279.2 2.0 fusion.2
  281.2 0.0 reduce-scatter.2.cloned.1.call-start
  281.2 78.7 %all-gather.2.cloned.1.call-done = bf16[8192,512]{1,0:T(8,128)(2,1)} async-done(((bf16[128,512]{1,0:T(8,128)(2,1)}), bf16[8192,512]{1,0:T(8,128)(2,1)}) %all-gather.2.cloned.1.call-update) | async-done | bytes 8388624 | tf_op jit(solution)/shard_map/all_gather | solution.py:49
  359.9 8.9 %gather_fusion = bf16[64,128,512]{2,1,0:T(8,128)(2,1)} fusion(bf16[64,128,512]{2,1,0:T(8,128)(2,1)} %bitcast.26, s32[1024]{0:T(1024)S(1)} %pad_clamp_fusion), kind=kCustom, calls=%fused_computation | custom fusion | bytes 16777472 | tf_op jit(solution)/shard_map/gather | solution.py:50
  368.8 8.3 %multiply_reduce_fusion = bf16[512,128]{1,0:T(8,128)(2,1)} fusion(bf16[64,128,512]{2,1,0:T(8,128)(2,1)} %gather_fusion, bf16[64,128,128]{2,1,0:T(8,128)(2,1)S(1)} %copy-done, f32[64]{0:T(128)S(1)} %convert_rsqrt_fusion), kind=kOutput, calls=%fused_computation.2 | convolution fusion | flops 1082064896 | bytes 10617088 | tf_op jit(solution)/shard_map/tij,tif->tjf/dot_general | solution.py:52
  377.1 0.7 fusion
  377.8 114.2 %all-reduce.5.cloned.1.call-done = f32[512,256]{1,0:T(8,128)} async-done(((f32[512,256]{1,0:T(8,128)}), f32[512,256]{1,0:T(8,128)}) %all-reduce.5.cloned.1.call-update) | async-done | bytes 524304 | tf_op jit(solution)/shard_map/psum | solution.py:47
  492.0 1.9 broadcast_multiply_fusion
  493.9 7.9 %reduce-scatter.2.cloned.1.call-done = bf16[128,256]{0,1:T(8,128)(2,1)} async-done(((bf16[128,512]{0,1:T(8,128)(2,1)}), bf16[128,256]{0,1:T(8,128)(2,1)}) %reduce-scatter.2.cloned.1.call-update) | async-done | bytes 65552 | tf_op jit(solution)/shard_map/reduce_scatter | solution.py:56
  501.8 1.6 copy.14
  (13 shorter events, 0.1 us)
Async XLA Ops:
  7.2 2.4 copy-start
  7.2 269.7 %all-reduce.3.cloned.1.call-start = ((), (), s32[]{:S(2)}) async-start(), calls=%async_computation.2 | async-start | bytes 262144 | tf_op jit(solution)/shard_map/psum | solution.py:38
  243.7 33.2 %copy-start.1 = (bf16[512,512]{1,0:T(8,128)(2,1)S(1)}, bf16[512,512]{1,0:T(8,128)(2,1)}, u32[]{:S(2)}) copy-start(bf16[512,512]{1,0:T(8,128)(2,1)} %param.11) | copy-start | bytes 1572868
  243.7 33.2 %copy-start.2 = (bf16[128,512]{1,0:T(8,128)(2,1)S(1)}, bf16[128,512]{1,0:T(8,128)(2,1)}, u32[]{:S(2)}) copy-start(bf16[128,512]{1,0:T(8,128)(2,1)} %param.13) | copy-start | bytes 393220
  243.7 33.2 %copy-start.3 = (f32[512]{0:T(512)S(1)}, f32[512]{0:T(512)}, u32[]{:S(2)}) copy-start(f32[512]{0:T(512)} %param.12) | copy-start | bytes 6148
  253.4 106.5 %all-gather.2.cloned.1.call-start = ((), (), s32[]{:S(2)}) async-start(), calls=%async_computation.4 | async-start | bytes 8519680 | tf_op jit(solution)/shard_map/all_gather | solution.py:49
  279.1 212.9 %all-reduce.5.cloned.1.call-start = ((), (), s32[]{:S(2)}) async-start(), calls=%async_computation.3 | async-start | bytes 1048576 | tf_op jit(solution)/shard_map/psum | solution.py:47
  281.2 220.6 %reduce-scatter.2.cloned.1.call-start = ((), (), s32[]{:S(2)}) async-start(), calls=%async_computation.5 | async-start | bytes 196608 | tf_op jit(solution)/shard_map/reduce_scatter | solution.py:56
Sparse Core Ops, SparseCore 0:
  253.6 23.3 all-reduce.2
  279.8 80.0 all-gather.1
  365.2 126.7 all-reduce.4
  494.3 7.4 reduce-scatter.1
where the time goes:
time: 512 us; the launch traced here: 510 us
  waiting for transfers between devices  224 us (44%)
  blocking collectives  200 us (39%)
  local copies, waits for them, and re-layouts  38.5 us (8%)
  matrix products  18.9 us (4%)
  other arithmetic  14.6 us (3%)
  between operations  13.8 us (3%)
    all_to_all x1, blocking collectives, per_device(): lax.all_to_all(send_buf.reshape(domains, slots, block, width), 'dom', spl...  200 us
    psum x1, waiting for transfers between devices, per_device(): lax.psum(weight_part, 'dom') / jnp.sqrt(jnp.float32(domains * block))  114 us
    all_gather x1, waiting for transfers between devices, per_device(): lax.all_gather(row_grad, 'dom', axis=0, tiled=True)  78.7 us
    psum x1, waiting for transfers between devices, per_device(): aggregated = lax.psum(partial_rows.astype(jnp.bfloat16), 'rep')  23.4 us
    scatter x1, local copies, waits for them, and re-layouts, per_device(): send_buf = jnp.zeros((domains * slots, block, width), jnp.bfloat16).at[sl...  22.1 us
  transfers between devices with their start and end apart: 4, of which 4 were waited for; matrix products, arithmetic and copies ran while one was open for 4% of the time, Pallas kernels for 0%

commit v1 on v0

v1 whole, which is shorter than its diff:
```python
import jax
import jax.numpy as jnp
from jax import lax
from jax.experimental import pallas as pl
from jax.experimental.pallas import tpu as pltpu
from jax.sharding import PartitionSpec as P


def build_blocks(dest_ref, count_ref, tiles_ref, out_ref, which, used):
    blocks = out_ref.shape[0]

    @pl.loop(0, blocks)
    def _(b):
        used[b] = 0
        which[2 * b] = 0
        which[2 * b + 1] = 0

    @pl.loop(0, tiles_ref.shape[0])
    def _(t):
        d = dest_ref[t]
        k = used[d]
        which[2 * d + k] = t
        used[d] = k + 1

    @pl.loop(0, blocks)
    def _(b):
        n = used[b]
        total = jnp.zeros(out_ref.shape[1:], jnp.float32)
        for k in range(2):
            t = which[2 * b + k]
            c = jnp.full((8, 128), jnp.maximum(count_ref[t], 1), jnp.int32).astype(jnp.float32)
            s = jnp.where(n > k, lax.rsqrt(c), 0.0)[0:1, :]
            total = total + tiles_ref[t].astype(jnp.float32) * s
        out_ref[b] = total.astype(out_ref.dtype)


def adjacency(tiles, dest, count, domains):
    shape = (domains,) + tiles.shape[1:]
    return pl.pallas_call(
        build_blocks,
        out_shape=jax.ShapeDtypeStruct(shape, jnp.bfloat16),
        in_specs=[
            pl.BlockSpec(memory_space=pltpu.SMEM),
            pl.BlockSpec(memory_space=pltpu.SMEM),
            pl.BlockSpec(memory_space=pltpu.VMEM),
        ],
        out_specs=pl.BlockSpec(memory_space=pltpu.VMEM),
        scratch_shapes=[pltpu.SMEM((2 * domains,), jnp.int32), pltpu.SMEM((domains,), jnp.int32)],
        name="adjacency",
    )(dest, count, tiles)


def per_device(features, tiles, tile_dest, tile_count, weight, bias, cotangent):
    domains = lax.axis_size("dom")
    r = lax.axis_index("rep")
    block, width = features.shape
    half = width // 2
    own = adjacency(tiles, tile_dest[:, 0], tile_count, domains)
    both = lax.all_gather(own, "rep", axis=0)
    feat = lax.dynamic_slice_in_dim(features, r * half, half, 1)
    partial = jnp.einsum("rbij,jf->bif", both, feat, preferred_element_type=jnp.float32)
    received = lax.all_to_all(
        partial.astype(jnp.bfloat16), "dom", split_axis=0, concat_axis=0, tiled=True
    )
    agg_half = jnp.sum(received, axis=0, dtype=jnp.float32).astype(jnp.bfloat16)
    agg = lax.all_gather(agg_half, "rep", axis=1, tiled=True)
    pre = jnp.dot(agg, weight, preferred_element_type=jnp.float32) + bias
    sig = jax.nn.sigmoid(pre)
    activated = lax.dynamic_slice_in_dim(pre * sig, r * half, half, 1).astype(jnp.bfloat16)
    pre_grad = (cotangent.astype(jnp.float32) * sig * (1.0 + pre * (1.0 - sig))).astype(
        jnp.bfloat16
    )
    grad_half = lax.dynamic_slice_in_dim(pre_grad, r * half, half, 1)
    w_half = lax.dynamic_slice_in_dim(weight, r * half, half, 0)
    row_grad = lax.dot_general(
        pre_grad, w_half, (((1,), (1,)), ((), ())), preferred_element_type=jnp.float32
    ).astype(jnp.bfloat16)
    every = lax.all_gather(row_grad, "dom", axis=0, tiled=True).reshape(domains, block, half)
    weight_part = jnp.dot(agg.T, grad_half, preferred_element_type=jnp.float32)
    weight_grad = lax.psum(weight_part, "dom") / jnp.sqrt(jnp.float32(domains * block))
    back = jnp.einsum("rbij,bif->jf", both, every, preferred_element_type=jnp.float32)
    return (activated, weight_grad, back.astype(jnp.bfloat16))


def solution(mesh):
    in_specs = (
        P("dom", None),
        P(("rep", "dom"), None, None),
        P(("rep", "dom"), None),
        P(("rep", "dom")),
        P(),
        P(),
        P("dom", None),
    )
    out_specs = (P("dom", "rep"), P(None, "rep"), P("dom", "rep"))
    return jax.shard_map(
        per_device, mesh=mesh, in_specs=in_specs, out_specs=out_specs, check_vma=False
    )
```

time: 512 us -> 312 us (0.61)
  blocking collectives: 200 us -> 65.9 us
  local copies, waits for them, and re-layouts: 38.5 us -> 0.02 us
  waiting for transfers between devices: 224 us -> 210 us
  matrix products: 18.9 us -> 7.27 us
  other arithmetic: 14.6 us -> 8.45 us
  Pallas kernels: 0 us -> 5.8 us
    all_to_all x1, blocking collectives: 200 us -> 64 us  [per_device(): lax.all_to_all(partial.astype(jnp.bfloat16), 'dom', split_axis=0, concat_...]
    psum x1 -> x0, waiting for transfers between devices: 23.4 us -> none  [per_device(): aggregated = lax.psum(partial_rows.astype(jnp.bfloat16), 'rep')]
    scatter x1 -> x0, local copies, waits for them, and re-layouts: 22.1 us -> none  [per_device(): send_buf = jnp.zeros((domains * slots, block, width), jnp.bfloat16).at[sl...]
    all_gather x0 -> x1, waiting for transfers between devices: none -> 18.9 us  [per_device(): both = lax.all_gather(own, 'rep', axis=0)]
    dot_general x5, matrix products: 18.9 us -> 7.27 us  [the longest x1 3.8 us: per_device(): jnp.einsum('rbij,bif->jf', both, every, preferred_element_type=jnp.float32)]
    all_gather x1, waiting for transfers between devices: 78.7 us -> 68.5 us  [per_device(): lax.all_gather(row_grad, 'dom', axis=0, tiled=True)]
    gather x1 -> x0, local copies, waits for them, and re-layouts: 8.9 us -> none  [per_device(): picked = every_grad[dest]]
    psum x1, waiting for transfers between devices: 114 us -> 122 us  [per_device(): lax.psum(weight_part, 'dom') / jnp.sqrt(jnp.float32(domains * block))]
  transfers between devices with their start and end apart: 4 -> 3, of which waited for: 4 -> 3; matrix products, arithmetic and copies ran while one was open for 4% -> 1% of each run, Pallas kernels for 0% -> 0%
where the time goes in v1:
time: 312 us; the launch traced here: 311 us
  waiting for transfers between devices  210 us (67%)
  blocking collectives  65.9 us (21%)
  between operations  13.8 us (4%)
  other arithmetic  8.45 us (3%)
  matrix products  7.27 us (2%)
  Pallas kernels  5.8 us (2%)
    psum x1, waiting for transfers between devices, per_device(): lax.psum(weight_part, 'dom') / jnp.sqrt(jnp.float32(domains * block))  122 us
    all_gather x1, waiting for transfers between devices, per_device(): lax.all_gather(row_grad, 'dom', axis=0, tiled=True)  68.5 us
    all_to_all x1, blocking collectives, per_device(): lax.all_to_all(partial.astype(jnp.bfloat16), 'dom', split_axis=0, concat_...  64 us
    all_gather x1, waiting for transfers between devices, per_device(): both = lax.all_gather(own, 'rep', axis=0)  18.9 us
  transfers between devices with their start and end apart: 3, of which 3 were waited for; matrix products, arithmetic and copies ran while one was open for 1% of the time, Pallas kernels for 0%

profile of v1, /device:TPU:0, one launch (start us, length us, event | category | flops | bytes accessed | tf_op | source)
XLA Modules:
  0.0 311.2 jit_solution(11536520041359148417)
XLA Ops:
  7.2 0.0 copy-start
  7.2 0.0 all-gather.6.cloned.1.call-start
  7.2 5.8 %adjacency.1 = bf16[64,128,128]{2,1,0:T(8,128)(2,1)} custom-call(s32[64]{0:T(128)} %bitcast.20, s32[64]{0:T(128)} %count_ref.1, bf16[64,128,128]{2,1,0:T(8,128)(2,1)} %tiles_ref.1), custom_call_target="tpu_custom_call" | custom-call | tf_op jit(solution)/shard_map/adjacency/pallas_call | solution.py:39
  13.0 0.0 all-gather.6.cloned.1.call-update
  13.1 0.0 all-reduce.2.cloned.1.call-start
  13.1 18.9 %all-gather.6.cloned.1.call-done = bf16[128,128,128]{2,1,0:T(8,128)(2,1)} async-done(((bf16[64,128,128]{2,1,0:T(8,128)(2,1)}), bf16[128,128,128]{2,1,0:T(8,128)(2,1)}) %all-gather.6.cloned.1.call-update) | async-done | bytes 4194320 | tf_op jit(solution)/shard_map/all_gather | solution.py:59
  32.0 3.1 convert_reduce_fusion
  35.1 0.0 copy-done.1
  35.1 1.2 convolution_convert_fusion
  36.4 64.0 %all_to_all.5 = bf16[64,128,256]{2,1,0:T(8,128)(2,1)} all-to-all(bf16[64,128,256]{2,1,0:T(8,128)(2,1)S(1)} %convolution_convert_fusion), channel_id=1, replica_groups=mesh['rep'=2,'dom'=64] {'dom'}, dimensions={0} | all-to-all | bytes 8388608 | tf_op jit(solution)/shard_map/all_to_all | solution.py:62
  100.3 2.8 reduce_sum.26
  103.2 1.9 all_gather.14
  105.1 0.0 copy-done.3
  105.1 0.3 multiply_convert_fusion
  105.4 1.0 fusion.4
  106.4 0.0 all-reduce.2.cloned.1.call-update
  106.5 0.0 all-gather.4.cloned.1.call-start
  106.5 0.9 convolution_convert_fusion.1
  107.4 0.0 all-gather.4.cloned.1.call-update
  107.4 0.7 fusion.2
  108.1 122.4 %all-reduce.2.cloned.1.call-done = f32[512,256]{1,0:T(8,128)} async-done(((f32[512,256]{1,0:T(8,128)}), f32[512,256]{1,0:T(8,128)}) %all-reduce.2.cloned.1.call-update) | async-done | bytes 524304 | tf_op jit(solution)/shard_map/psum | solution.py:80
  230.5 1.9 broadcast_multiply_fusion
  232.4 68.5 %all-gather.4.cloned.1.call-done = bf16[8192,256]{1,0:T(8,128)(2,1)} async-done(((bf16[128,256]{1,0:T(8,128)(2,1)}), bf16[8192,256]{1,0:T(8,128)(2,1)}) %all-gather.4.cloned.1.call-update) | async-done | bytes 4194320 | tf_op jit(solution)/shard_map/all_gather | solution.py:78
  300.9 3.8 %fusion = bf16[128,256]{1,0:T(8,128)(2,1)} fusion(bf16[64,128,128]{2,1,0:T(8,128)(2,1)S(1)} %convert_reduce_fusion, bf16[64,128,256]{2,1,0:T(8,128)(2,1)} %bitcast.19), kind=kOutput, calls=%fused_computation.4 | convolution fusion | flops 536870912 | bytes 6356992 | tf_op jit(solution)/shard_map/rbij,bif->jf/dot_general | solution.py:81
  (5 shorter events, 0.0 us)
Async XLA Ops:
  7.2 97.9 %copy-start = (bf16[512,512]{1,0:T(8,128)(2,1)S(1)}, bf16[512,512]{1,0:T(8,128)(2,1)}, u32[]{:S(2)}) copy-start(bf16[512,512]{1,0:T(8,128)(2,1)} %param.11) | copy-start | bytes 1572868
  7.2 24.8 %all-gather.6.cloned.1.call-start = ((), (), s32[]{:S(2)}) async-start(), calls=%async_computation.3 | async-start | bytes 6291456 | tf_op jit(solution)/shard_map/all_gather | solution.py:59
  13.0 22.1 %copy-start.1 = (bf16[128,512]{1,0:T(8,128)(2,1)S(1)}, bf16[128,512]{1,0:T(8,128)(2,1)}, u32[]{:S(2)}) copy-start(bf16[128,512]{1,0:T(8,128)(2,1)} %param.7) | copy-start | bytes 393220
  13.1 217.5 %all-reduce.2.cloned.1.call-start = ((), (), s32[]{:S(2)}) async-start(), calls=%async_computation.1 | async-start | bytes 1048576 | tf_op jit(solution)/shard_map/psum | solution.py:80
  100.3 4.7 %copy-start.2 = (bf16[128,512]{1,0:T(8,128)(2,1)S(1)}, bf16[128,512]{1,0:T(8,128)(2,1)}, u32[]{:S(2)}) copy-start(bf16[128,512]{1,0:T(8,128)(2,1)} %param.13) | copy-start | bytes 393220
  100.3 4.7 %copy-start.3 = (f32[512]{0:T(512)S(1)}, f32[512]{0:T(512)}, u32[]{:S(2)}) copy-start(f32[512]{0:T(512)} %param.12) | copy-start | bytes 6148
  106.5 194.4 %all-gather.4.cloned.1.call-start = ((), (), s32[]{:S(2)}) async-start(), calls=%async_computation.2 | async-start | bytes 4259840 | tf_op jit(solution)/shard_map/all_gather | solution.py:78
Sparse Core Ops, SparseCore 0:
  13.2 18.7 all-gather.5
  106.6 123.8 all-reduce.1
  234.4 66.4 all-gather.3

commit v2 on v1

v2 whole, which is shorter than its diff:
```python
import math

import jax
import jax.numpy as jnp
from jax import lax
from jax.experimental import pallas as pl
from jax.experimental.pallas import tpu as pltpu
from jax.sharding import PartitionSpec as P


def build_blocks(dest_ref, count_ref, tiles_ref, out_ref, which, used):
    blocks = out_ref.shape[0]

    @pl.loop(0, blocks)
    def _(b):
        used[b] = 0
        which[2 * b] = 0
        which[2 * b + 1] = 0

    @pl.loop(0, tiles_ref.shape[0])
    def _(t):
        d = dest_ref[t]
        k = used[d]
        which[2 * d + k] = t
        used[d] = k + 1

    @pl.loop(0, blocks)
    def _(b):
        n = used[b]
        total = jnp.zeros(out_ref.shape[1:], jnp.float32)
        for k in range(2):
            t = which[2 * b + k]
            c = jnp.full((8, 128), jnp.maximum(count_ref[t], 1), jnp.int32).astype(jnp.float32)
            s = jnp.where(n > k, lax.rsqrt(c), 0.0)[0:1, :]
            total = total + tiles_ref[t].astype(jnp.float32) * s
        out_ref[b] = total.astype(out_ref.dtype)


def adjacency(tiles, dest, count, domains):
    shape = (domains,) + tiles.shape[1:]
    return pl.pallas_call(
        build_blocks,
        out_shape=jax.ShapeDtypeStruct(shape, jnp.bfloat16),
        in_specs=[
            pl.BlockSpec(memory_space=pltpu.SMEM),
            pl.BlockSpec(memory_space=pltpu.SMEM),
            pl.BlockSpec(memory_space=pltpu.VMEM),
        ],
        out_specs=pl.BlockSpec(memory_space=pltpu.VMEM),
        scratch_shapes=[pltpu.SMEM((2 * domains,), jnp.int32), pltpu.SMEM((domains,), jnp.int32)],
        name="adjacency",
    )(dest, count, tiles)


ROWS = ((0, 48), (48, 48), (96, 32))
STRIDE = (16, 4, 1)
MESH = pl.DeviceIdType.MESH


def layer_kernel(
    own_ref, feat_ref, weight_ref, bias_ref, cot_ref,
    act_ref, wgrad_ref, fgrad_ref,
    a2, at0, at1, at2, ff, p0, p1, p2, g0, g1, g2,
    ra0, ra1, ra2, rb0, rb1, rb2, rc0, rc1, rc2,
    agg, pg, actv, wp, wra, wrb, wrc, wg, acc,
    own_sem, swap_send, swap_recv, agg_send, agg_recv,
    rs_send, rs_recv, ag_send, ag_recv, ws_send, ws_recv, wa_send, wa_recv,
):
    r = lax.axis_index("rep")
    d = lax.axis_index("dom")
    other = 1 - r
    me = (d // 16, (d // 4) % 4, d % 4)
    P_ = (p0, p1, p2)
    G_ = (g0, g1, g2)
    AT = (at0, at1, at2)
    RV = ((ra0, ra1, ra2), (rb0, rb1, rb2), (rc0, rc1, rc2))
    f32, bf16 = jnp.float32, jnp.bfloat16
    started = []

    def near(a, o):
        c = (me[a] + o) % 4
        return c, (r, d + (c - me[a]) * STRIDE[a])

    barrier = pltpu.get_barrier_semaphore()
    pl.semaphore_signal(barrier, inc=1, device_id=(other, d), device_id_type=MESH)
    for a in range(3):
        for o in (1, 2, 3):
            pl.semaphore_signal(barrier, inc=1, device_id=near(a, o)[1], device_id_type=MESH)
    pl.semaphore_wait(barrier, 10)

    def remote(src, dst, ssem, rsem, dev):
        c = pltpu.make_async_remote_copy(
            src_ref=src, dst_ref=dst, send_sem=ssem, recv_sem=rsem,
            device_id=dev, device_id_type=MESH,
        )
        c.start()
        started.append(c)
        return c

    half = 256
    cols = pl.ds(pl.multiple_of(r * half, half), half)
    swaps, locals_ = [], []
    for i in range(4):
        swaps.append(
            remote(own_ref.at[i], a2.at[i, :, :, :, 128:256], swap_send.at[i], swap_recv.at[i], (other, d))
        )
        c = pltpu.make_async_copy(own_ref.at[i], a2.at[i, :, :, :, 0:128], own_sem.at[i])
        c.start()
        locals_.append(c)
    ff[0:128, :] = feat_ref[:, cols]
    ff[128:256, :] = feat_ref[:, cols]

    for i in range(4):
        locals_[i].wait()
        swaps[i].wait_recv()

        def forward(j, _):
            lhs = a2[i, j].reshape(512, 256)
            res = jnp.dot(lhs, ff[...], preferred_element_type=f32).astype(bf16)
            res = res.reshape(4, 128, 256)
            for k, (lo, n) in enumerate(ROWS):
                for h in range(2):
                    P_[k][i, j, :, h] = res[:, lo : lo + n, 128 * h : 128 * h + 128]
            return 0

        lax.fori_loop(0, 4, forward, 0)

    def view(fixed, h):
        return tuple(fixed.get(a, slice(None)) for a in range(3)) + (h,)

    def rs_open(k, j):
        axes = [(k + i) % 3 for i in range(3)]
        a = axes[j]
        fixed = {axes[i]: me[axes[i]] for i in range(j)}
        rv = RV[j][k]
        src = P_[k]
        out = []
        for w, (sign, h1) in enumerate(((1, 0), (3, 1))):
            c1, dev = near(a, sign)
            c2, _ = near(a, 2)
            first = remote(
                src.at[view({**fixed, a: c2}, h1)], rv.at[w, 0],
                rs_send.at[k, j, w, 0], rs_recv.at[k, j, w, 0], dev,
            )
            second = remote(
                src.at[view({**fixed, a: c1}, 1 - h1)], rv.at[w, 1],
                rs_send.at[k, j, w, 1], rs_recv.at[k, j, w, 1], dev,
            )
            out.append((first, second, view({**fixed, a: c1}, h1), dev))
        return out

    def rs_pass(k, j, opened):
        rv = RV[j][k]
        src = P_[k]
        for w in range(2):
            first, second, where, dev = opened[w]
            first.wait_recv()
            src[where] = (src[where].astype(f32) + rv[w, 0].astype(f32)).astype(bf16)
            third = remote(
                src.at[where], rv.at[w, 2], rs_send.at[k, j, w, 2], rs_recv.at[k, j, w, 2], dev
            )
            opened[w] = (second, third)

    def rs_close(k, j, opened):
        rv = RV[j][k]
        src = P_[k]
        axes = [(k + i) % 3 for i in range(3)]
        fixed = {axes[i]: me[axes[i]] for i in range(j + 1)}
        for w in range(2):
            for c in opened[w]:
                c.wait_recv()
        for h in range(2):
            where = view(fixed, h)
            total = src[where].astype(f32) + rv[h, 2].astype(f32) + rv[1 - h, 1].astype(f32)
            if j < 2:
                src[where] = total.astype(bf16)
            else:
                lo, n = ROWS[k]
                agg[lo : lo + n, pl.ds(pl.multiple_of(r * half + 128 * h, 128), 128)] = total.astype(bf16)

    opened = [rs_open(k, 0) for k in range(3)]
    for k in range(3):
        for c in range(4):
            sel = tuple(c if a == k else slice(None) for a in range(3)) + (slice(*(ROWS[k][0], sum(ROWS[k]))),)
            AT[k][c] = a2[sel].reshape(16 * ROWS[k][1], 256).T
    for j in range(3):
        if j > 0:
            opened = [rs_open(k, j) for k in range(3)]
        for k in range(3):
            rs_pass(k, j, opened[k])
        for k in range(3):
            rs_close(k, j, opened[k])

    mine = agg.at[:, cols]
    swap = remote(mine, mine, agg_send.at[0], agg_recv.at[0], (other, d))
    swap.wait_recv()
    pre = jnp.dot(agg[...], weight_ref[...], preferred_element_type=f32) + bias_ref[...]
    sig = jax.nn.sigmoid(pre)
    pg[...] = (cot_ref[...].astype(f32) * sig * (1.0 + pre * (1.0 - sig))).astype(bf16)
    actv[...] = (pre * sig).astype(bf16)
    row_grad = lax.dot_general(
        pg[...], weight_ref[cols, :], (((1,), (1,)), ((), ())), preferred_element_type=f32
    ).astype(bf16)
    for k, (lo, n) in enumerate(ROWS):
        for h in range(2):
            G_[k][me[0], me[1], me[2], h] = row_grad[lo : lo + n, 128 * h : 128 * h + 128]

    def ag_axes(k, j):
        axes = [(k + 2 - i) % 3 for i in range(3)]
        return axes[j], {axes[i]: me[axes[i]] for i in range(j + 1, 3)}

    def ag_open(k, j):
        a, fixed = ag_axes(k, j)
        out = []
        for w, (sign, h1) in enumerate(((1, 0), (3, 1))):
            _, dev = near(a, sign)
            c = []
            for m, h in enumerate((h1, 1 - h1)):
                ref = G_[k].at[view({**fixed, a: me[a]}, h)]
                c.append(remote(ref, ref, ag_send.at[k, j, w, m], ag_recv.at[k, j, w, m], dev))
            out.append(c)
        return out

    def ag_pass(k, j, opened):
        a, fixed = ag_axes(k, j)
        for w, (sign, h1) in enumerate(((1, 0), (3, 1))):
            _, dev = near(a, sign)
            origin, _ = near(a, 4 - sign)
            opened[w][0].wait_recv()
            ref = G_[k].at[view({**fixed, a: origin}, h1)]
            opened[w].append(remote(ref, ref, ag_send.at[k, j, w, 2], ag_recv.at[k, j, w, 2], dev))

    def ag_close(k, j, opened):
        for w in range(2):
            opened[w][1].wait_recv()
        for w in range(2):
            opened[w][2].wait_recv()

    WR = (wra, wrb, wrc)
    WS_AXES = (0, 1, 2)
    WA_AXES = (0, 2, 1)

    def wview(fixed):
        return tuple(fixed.get(a, slice(None)) for a in range(3))

    def ws_open(j):
        a = WS_AXES[j]
        fixed = {WS_AXES[i]: me[WS_AXES[i]] for i in range(j)}
        out = []
        for o in (1, 3, 2):
            c, dev = near(a, o)
            out.append(
                remote(wp.at[wview({**fixed, a: c})], WR[j].at[o - 1], ws_send.at[j, o - 1], ws_recv.at[j, o - 1], dev)
            )
        return out

    def ws_close(j, opened):
        for c in opened:
            c.wait_recv()
        where = wview({WS_AXES[i]: me[WS_AXES[i]] for i in range(j + 1)})
        total = wp[where].astype(f32)
        for o in range(3):
            total = total + WR[j][o].astype(f32)
        (wp if j < 2 else wg)[where] = total.astype(bf16)

    def wa_open(j):
        a = WA_AXES[j]
        fixed = {WA_AXES[i]: me[WA_AXES[i]] for i in range(j, 3)}
        ref = wg.at[wview(fixed)]
        out = []
        for o in (1, 3, 2):
            _, dev = near(a, o)
            out.append(remote(ref, ref, wa_send.at[j, o - 1], wa_recv.at[j, o - 1], dev))
        return out

    def wa_close(opened):
        for c in opened:
            c.wait_recv()

    gather = [ag_open(k, 0) for k in range(3)]
    part = lax.dot_general(
        agg[...], pg[:, cols], (((0,), (0,)), ((), ())), preferred_element_type=f32
    ).astype(bf16)
    for h in range(2):
        wp[2 * h : 2 * h + 2] = part[:, 128 * h : 128 * h + 128].reshape(2, 4, 4, 16, 128)
    w = ws_open(0)
    act_ref[...] = actv[:, cols]
    for k in range(3):
        ag_pass(k, 0, gather[k])
    for k in range(3):
        ag_close(k, 0, gather[k])
    gather = [ag_open(k, 1) for k in range(3)]
    ws_close(0, w)
    w = ws_open(1)
    for k in range(3):
        ag_pass(k, 1, gather[k])
    ws_close(1, w)
    w = ws_open(2)
    for k in range(3):
        ag_close(k, 1, gather[k])
    gather = [ag_open(k, 2) for k in range(3)]
    ws_close(2, w)
    w = wa_open(0)

    acc[...] = jnp.zeros_like(acc)

    def backward(k, o):
        c, _ = near(k, o)
        n = 16 * ROWS[k][1]
        lhs = AT[k][c]
        for h in range(2):
            rhs = G_[k][view({k: c}, h)].reshape(n, 128)
            acc[:, 128 * h : 128 * h + 128] += jnp.dot(lhs, rhs, preferred_element_type=f32)

    for k in range(3):
        ag_pass(k, 2, gather[k])
    wa_close(w)
    w = wa_open(1)
    for k in range(3):
        backward(k, 0)
    for k in range(3):
        for q in range(2):
            gather[k][q][1].wait_recv()
    wa_close(w)
    w = wa_open(2)
    for k in range(3):
        backward(k, 1)
        backward(k, 3)
    for k in range(3):
        for q in range(2):
            gather[k][q][2].wait_recv()
    for k in range(3):
        backward(k, 2)
    fgrad_ref[...] = (acc[0:128, :] + acc[128:256, :]).astype(bf16)
    wa_close(w)
    norm = 1.0 / math.sqrt(8192.0)
    for h in range(2):
        full = wg[2 * h : 2 * h + 2].reshape(512, 128).astype(f32) * norm
        wgrad_ref[:, 128 * h : 128 * h + 128] = full
    for c in started:
        c.wait_send()


def layer(own, feat, weight, bias, cot):
    bf16, f32 = jnp.bfloat16, jnp.float32
    V = pltpu.VMEM
    dma = pltpu.SemaphoreType.DMA
    sizes = [n for _, n in ROWS]
    scratch = [V((4, 4, 4, 128, 256), bf16)]
    scratch += [V((4, 256, 16 * n), bf16) for n in sizes]
    scratch += [V((256, 256), bf16)]
    scratch += [V((4, 4, 4, 2, n, 128), bf16) for n in sizes]
    scratch += [V((4, 4, 4, 2, n, 128), bf16) for n in sizes]
    scratch += [V((2, 3, 4, 4, n, 128), bf16) for n in sizes]
    scratch += [V((2, 3, 4, n, 128), bf16) for n in sizes]
    scratch += [V((2, 3, n, 128), bf16) for n in sizes]
    scratch += [V((128, 512), bf16)] * 3
    scratch += [V((4, 4, 4, 16, 128), bf16)]
    scratch += [V((3, 4, 4, 16, 128), bf16), V((3, 4, 16, 128), bf16), V((3, 16, 128), bf16)]
    scratch += [V((4, 4, 4, 16, 128), bf16), V((256, 256), f32)]
    scratch += [dma((4,)), dma((4,)), dma((4,)), dma((1,)), dma((1,))]
    scratch += [dma((3, 3, 2, 3))] * 4 + [dma((3, 3))] * 4
    whole = pl.BlockSpec(memory_space=pltpu.VMEM)
    return pl.pallas_call(
        layer_kernel,
        out_shape=[
            jax.ShapeDtypeStruct((128, 256), bf16),
            jax.ShapeDtypeStruct((512, 256), f32),
            jax.ShapeDtypeStruct((128, 256), bf16),
        ],
        in_specs=[pl.BlockSpec(memory_space=pl.ANY)] + [whole] * 4,
        out_specs=[whole] * 3,
        scratch_shapes=scratch,
        compiler_params=pltpu.CompilerParams(collective_id=0, has_side_effects=True),
        name="layer",
    )(own, feat, weight, bias, cot)


def per_device(features, tiles, tile_dest, tile_count, weight, bias, cotangent):
    domains = lax.axis_size("dom")
    own = adjacency(tiles, tile_dest[:, 0], tile_count, domains)
    own = own.reshape(4, 4, 4, 128, 128)
    act, wgrad, fgrad = layer(own, features, weight, bias.reshape(1, -1), cotangent)
    return act, wgrad, fgrad


def solution(mesh):
    in_specs = (
        P("dom", None),
        P(("rep", "dom"), None, None),
        P(("rep", "dom"), None),
        P(("rep", "dom")),
        P(),
        P(),
        P("dom", None),
    )
    out_specs = (P("dom", "rep"), P(None, "rep"), P("dom", "rep"))
    return jax.shard_map(
        per_device, mesh=mesh, in_specs=in_specs, out_specs=out_specs, check_vma=False
    )
```

time: 312 us -> 93.2 us (0.30)
  waiting for transfers between devices: 210 us -> 0 us
  Pallas kernels: 5.8 us -> 87.4 us
  blocking collectives: 65.9 us -> 0 us
  between operations: 13.8 us -> 0.64 us
  other arithmetic: 8.45 us -> 0 us
  matrix products: 7.27 us -> 0 us
  local copies, waits for them, and re-layouts: 0.02 us -> 4.81 us
    psum x1 -> x0, waiting for transfers between devices: 122 us -> none  [per_device(): lax.psum(weight_part, 'dom') / jnp.sqrt(jnp.float32(domains * block))]
    all_gather x2 -> x0, waiting for transfers between devices: 87.4 us -> none  [the longest x1 68.5 us: per_device(): lax.all_gather(row_grad, 'dom', axis=0, tiled=True)]
    pallas_call x0 -> x1, Pallas kernels: none -> 81.6 us  [layer(): pl.pallas_call(layer_kernel, out_shape=[jax.ShapeDtypeStruct((128, 256),...]
    all_to_all x1 -> x0, blocking collectives: 64 us -> none  [per_device(): lax.all_to_all(partial.astype(jnp.bfloat16), 'dom', split_axis=0, concat_...]
    dot_general x5 -> x0, matrix products: 7.27 us -> none  [the longest x1 3.8 us: per_device(): jnp.einsum('rbij,bif->jf', both, every, preferred_element_type=jnp.float32)]
    reduce_sum x2 -> x0, other arithmetic: 5.92 us -> none  [the longest x1 3.1 us: per_device(): jnp.einsum('rbij,jf->bif', both, feat, preferred_element_type=jnp.float32)]
    unnamed x8 -> x3, local copies, waits for them, and re-layouts: 0.02 us -> 4.81 us
  transfers between devices with their start and end apart: 3 -> 0, of which waited for: 3 -> 0; matrix products, arithmetic and copies ran while one was open for 1% -> 0% of each run, Pallas kernels for 0% -> 0%
where the time goes in v2:
time: 93.2 us; the launch traced here: 92.8 us
  Pallas kernels  87.4 us (94%)
  local copies, waits for them, and re-layouts  4.81 us (5%)
    pallas_call x1, Pallas kernels, layer(): pl.pallas_call(layer_kernel, out_shape=[jax.ShapeDtypeStruct((128, 256),...  81.6 us
    pallas_call x1, Pallas kernels, adjacency(): pl.pallas_call(build_blocks, out_shape=jax.ShapeDtypeStruct(shape, jnp.bf...  5.78 us
    unnamed x3, local copies, waits for them, and re-layouts  4.81 us

profile of v2, /device:TPU:0, one launch (start us, length us, event | category | flops | bytes accessed | tf_op | source)
XLA Modules:
  0.0 92.8 jit_solution(3610624188738059561)
XLA Ops:
  0.6 5.8 %adjacency.1 = bf16[64,128,128]{2,1,0:T(8,128)(2,1)} custom-call(s32[64]{0:T(128)} %bitcast.5, s32[64]{0:T(128)} %count_ref.1, bf16[64,128,128]{2,1,0:T(8,128)(2,1)} %tiles_ref.1), custom_call_target="tpu_custom_call" | custom-call | tf_op jit(solution)/shard_map/adjacency/pallas_call | solution.py:41
  6.4 81.6 %layer.1 = (bf16[128,256]{1,0:T(8,128)(2,1)}, f32[512,256]{1,0:T(8,128)}, bf16[128,256]{1,0:T(8,128)(2,1)}) custom-call(bf16[4,4,4,128,128]{4,3,2,1,0:T(8,128)(2,1)} %bitcast.3, bf16[128,512]{1,0:T(8,128)(2,1)} %feat_ref.1, bf16[512,512]{1,0:T(8,128)(2,1)} %weight_ref.1, f32[1,512]{1,0:T(1,128)} %bitcast.4, bf16[128,512]{1,0:T(8,128)(2,1)} %cot_ref.1), custom_call_target="tpu_custom_call" | custom-call | tf_op jit(solution)/shard_map/layer/pallas_call | solution.py:364
  88.0 1.5 %copy.13 = bf16[128,256]{1,0:T(8,128)(2,1)} copy(bf16[128,256]{1,0:T(8,128)(2,1)} %get-tuple-element.6) | data formatting | bytes 131072
  89.5 1.9 %copy.14 = f32[512,256]{1,0:T(8,128)} copy(f32[512,256]{1,0:T(8,128)} %get-tuple-element.7) | data formatting | bytes 1048576
  91.4 1.5 %copy.15 = bf16[128,256]{1,0:T(8,128)(2,1)} copy(bf16[128,256]{1,0:T(8,128)(2,1)} %get-tuple-element.8) | data formatting | bytes 131072

commit v3 on v2

v3 whole, which is shorter than its diff:
```python
import math

import jax
import jax.numpy as jnp
from jax import lax
from jax.experimental import pallas as pl
from jax.experimental.pallas import tpu as pltpu
from jax.sharding import PartitionSpec as P


def build_blocks(dest_ref, count_ref, tiles_ref, out_ref, which, used):
    blocks = out_ref.shape[0]

    @pl.loop(0, blocks)
    def _(b):
        used[b] = 0
        which[2 * b] = 0
        which[2 * b + 1] = 0

    @pl.loop(0, tiles_ref.shape[0], unroll=8)
    def _(t):
        d = dest_ref[t]
        k = used[d]
        which[2 * d + k] = t
        used[d] = k + 1

    @pl.loop(0, blocks, unroll=4)
    def _(b):
        n = used[b]
        total = jnp.zeros(out_ref.shape[1:], jnp.float32)
        for k in range(2):
            t = which[2 * b + k]
            c = jnp.full((8, 128), jnp.maximum(count_ref[t], 1), jnp.int32).astype(jnp.float32)
            s = jnp.where(n > k, lax.rsqrt(c), 0.0)[0:1, :]
            total = total + tiles_ref[t].astype(jnp.float32) * s
        out_ref[b] = total.astype(out_ref.dtype)


def adjacency(tiles, dest, count, domains):
    shape = (domains,) + tiles.shape[1:]
    return pl.pallas_call(
        build_blocks,
        out_shape=jax.ShapeDtypeStruct(shape, jnp.bfloat16),
        in_specs=[
            pl.BlockSpec(memory_space=pltpu.SMEM),
            pl.BlockSpec(memory_space=pltpu.SMEM),
            pl.BlockSpec(memory_space=pltpu.VMEM),
        ],
        out_specs=pl.BlockSpec(memory_space=pltpu.VMEM),
        scratch_shapes=[pltpu.SMEM((2 * domains,), jnp.int32), pltpu.SMEM((domains,), jnp.int32)],
        name="adjacency",
    )(dest, count, tiles)


ROWS = ((0, 48), (48, 48), (96, 32))
STRIDE = (16, 4, 1)
MESH = pl.DeviceIdType.MESH


def layer_kernel(
    own_ref, feat_ref, weight_ref, bias_ref, cot_ref,
    act_ref, wsum_ref, fgrad_ref,
    a2, at0, at1, at2, ff, p0, p1, p2, g0, g1, g2,
    ra0, ra1, ra2, rb0, rb1, rb2, rc0, rc1, rc2,
    agg, pg, actv, wp, wra, wrb, wrc, wg, acc,
    own_sem, swap_send, swap_recv, agg_send, agg_recv,
    rs_send, rs_recv, rd_send, rd_recv, ad_send, ad_recv,
    ag_send, ag_recv, ws_send, ws_recv, wa_send, wa_recv,
):
    r = lax.axis_index("rep")
    d = lax.axis_index("dom")
    other = 1 - r
    me = (d // 16, (d // 4) % 4, d % 4)
    P_ = (p0, p1, p2)
    G_ = (g0, g1, g2)
    AT = (at0, at1, at2)
    RV = ((ra0, ra1, ra2), (rb0, rb1, rb2), (rc0, rc1, rc2))
    f32, bf16 = jnp.float32, jnp.bfloat16
    started = []

    def near(a, o):
        c = (me[a] + o) % 4
        return c, (r, d + (c - me[a]) * STRIDE[a])

    barrier = pltpu.get_barrier_semaphore()
    pl.semaphore_signal(barrier, inc=1, device_id=(other, d), device_id_type=MESH)
    for a in range(3):
        for o in (1, 2, 3):
            pl.semaphore_signal(barrier, inc=1, device_id=near(a, o)[1], device_id_type=MESH)
    pl.semaphore_wait(barrier, 10)

    def remote(src, dst, ssem, rsem, dev):
        c = pltpu.make_async_remote_copy(
            src_ref=src, dst_ref=dst, send_sem=ssem, recv_sem=rsem,
            device_id=dev, device_id_type=MESH,
        )
        c.start()
        started.append(c)
        return c

    half = 256
    cols = pl.ds(pl.multiple_of(r * half, half), half)
    ORDER = (2, 1, 3, 0)
    WAYS = ((1, 0), (3, 1))
    swaps, locals_ = [], []
    for s, o in enumerate(ORDER):
        i, _ = near(0, o)
        swaps.append(
            remote(own_ref.at[i], a2.at[i, :, :, :, 128:256], swap_send.at[s], swap_recv.at[s], (other, d))
        )
        c = pltpu.make_async_copy(own_ref.at[i], a2.at[i, :, :, :, 0:128], own_sem.at[s])
        c.start()
        locals_.append(c)
    ff[0:128, :] = feat_ref[:, cols]
    ff[128:256, :] = feat_ref[:, cols]

    def view(fixed, h):
        return tuple(fixed.get(a, slice(None)) for a in range(3)) + ((h,) if h is not None else ())

    def rs_axes(k):
        return [(k + i) % 3 for i in range(3)]

    def rs_fixed(k, j):
        axes = rs_axes(k)
        return axes[j], {axes[i]: me[axes[i]] for i in range(j)}

    def rs_send_of(k, j, w, m, extra):
        a, fixed = rs_fixed(k, j)
        sign, h1 = WAYS[w]
        c, _ = near(a, 2 if m == 0 else sign)
        _, dev = near(a, sign)
        h = h1 if m == 0 else 1 - h1
        spot = rv_view(k, j, w, m, extra)
        return dict(
            src_ref=P_[k].at[view({**fixed, a: c, **extra}, h)], dst_ref=RV[j][k].at[spot],
            send_sem=rs_send.at[k, j, w, m], recv_sem=rs_recv.at[k, j, w, m],
            device_id=dev, device_id_type=MESH,
        )

    def rv_view(k, j, w, m, extra):
        a, fixed = rs_fixed(k, j)
        left = [x for x in range(3) if x != a and x not in fixed]
        return (w, m) + tuple(extra.get(x, slice(None)) for x in left)

    def rs_open(k, j, w, m, extra=None):
        pltpu.make_async_remote_copy(**rs_send_of(k, j, w, m, extra or {})).start()

    def rs_whole(k, j, w, m):
        c = pltpu.make_async_remote_copy(**rs_send_of(k, j, w, m, {}))
        started.append(c)
        return c

    lag = None
    for s, o in enumerate(ORDER):
        i, _ = near(0, o)
        locals_[s].wait()
        swaps[s].wait_recv()

        def forward(j, _, i=i):
            lhs = a2[i, j].reshape(512, 256)
            res = jnp.dot(lhs, ff[...], preferred_element_type=f32).astype(bf16)
            res = res.reshape(4, 128, 256)
            for k, (lo, n) in enumerate(ROWS):
                for h in range(2):
                    P_[k][i, j, :, h] = res[:, lo : lo + n, 128 * h : 128 * h + 128]
            return 0

        lax.fori_loop(0, 4, forward, 0)
        if o == 2:
            rs_open(0, 0, 0, 0)
            rs_open(0, 0, 1, 0)
        elif o == 1:
            rs_open(0, 0, 0, 1)
        elif o == 3:
            rs_open(0, 0, 1, 1)
        for k in (1, 2):
            for w in range(2):
                rs_open(k, 0, w, 0, {0: i})
        for k in (1, 2):
            for w in range(2):
                if lag is not None:
                    rs_open(k, 0, w, 1, {0: lag})
        lag = i
    for k in (1, 2):
        for w in range(2):
            rs_open(k, 0, w, 1, {0: lag})

    thirds = {}

    def rs_pass(k, j):
        a, fixed = rs_fixed(k, j)
        b = rs_axes(k)[j + 1]
        rv, src = RV[j][k], P_[k]
        for w in range(2):
            rs_whole(k, j, w, 0).wait_recv()
        for o in ORDER:
            p, _ = near(b, o)
            for w, (sign, h1) in enumerate(WAYS):
                c1, dev = near(a, sign)
                where = view({**fixed, a: c1, b: p}, h1)
                got = rv_view(k, j, w, 0, {b: p})
                src[where] = (src[where].astype(f32) + rv[got].astype(f32)).astype(bf16)
                thirds[k, j, w, o] = remote(
                    src.at[where], rv.at[rv_view(k, j, w, 2, {b: p})],
                    rs_send.at[k, j, w, 2 + o], rs_recv.at[k, j, w, 2 + o], dev,
                )

    direct = {}

    def rs_close(k, j, o):
        a, fixed = rs_fixed(k, j)
        b = rs_axes(k)[j + 1]
        rv, src = RV[j][k], P_[k]
        p, dev = near(b, o)
        for w in range(2):
            thirds[k, j, w, o].wait_recv()
        for h in range(2):
            where = view({**fixed, a: me[a], b: p}, h)
            one = rv[rv_view(k, j, h, 2, {b: p})]
            two = rv[rv_view(k, j, 1 - h, 1, {b: p})]
            src[where] = (src[where].astype(f32) + one.astype(f32) + two.astype(f32)).astype(bf16)
        if j == 1:
            if o > 0:
                direct[k, o] = remote(
                    src.at[view({**fixed, a: me[a], b: p}, None)], RV[2][k].at[o - 1],
                    rd_send.at[k, o - 1], rd_recv.at[k, o - 1], dev,
                )
        elif o == 2:
            rs_open(k, 1, 0, 0)
            rs_open(k, 1, 1, 0)
        elif o == 1:
            rs_open(k, 1, 0, 1)
        elif o == 3:
            rs_open(k, 1, 1, 1)

    def turn(k):
        for c in range(4):
            sel = tuple(c if a == k else slice(None) for a in range(3)) + (slice(*(ROWS[k][0], sum(ROWS[k]))),)
            AT[k][c] = a2[sel].reshape(16 * ROWS[k][1], 256).T

    turn(2)
    rs_pass(0, 0)
    turn(0)
    rs_pass(2, 0)
    rs_pass(1, 0)
    turn(1)
    for j in range(2):
        if j > 0:
            for k in range(3):
                rs_pass(k, j)
        for k in range(3):
            for w in range(2):
                rs_whole(k, j, w, 1).wait_recv()
        for o in ORDER:
            for k in range(3):
                rs_close(k, j, o)
    for k, (lo, n) in enumerate(ROWS):
        for o in (1, 3, 2):
            direct[k, o].wait_recv()
        for h in range(2):
            total = P_[k][me[0], me[1], me[2], h].astype(f32)
            for o in range(3):
                total = total + RV[2][k][o, h].astype(f32)
            agg[lo : lo + n, pl.ds(pl.multiple_of(r * half + 128 * h, 128), 128)] = total.astype(bf16)

    mine = agg.at[:, cols]
    swap = remote(mine, mine, agg_send.at[0], agg_recv.at[0], (other, d))
    swap.wait_recv()
    pre = jnp.dot(agg[...], weight_ref[...], preferred_element_type=f32) + bias_ref[...]
    sig = jax.nn.sigmoid(pre)
    pg[...] = (cot_ref[...].astype(f32) * sig * (1.0 + pre * (1.0 - sig))).astype(bf16)
    actv[...] = (pre * sig).astype(bf16)
    row_grad = lax.dot_general(
        pg[...], weight_ref[cols, :], (((1,), (1,)), ((), ())), preferred_element_type=f32
    ).astype(bf16)
    for k, (lo, n) in enumerate(ROWS):
        for h in range(2):
            G_[k][me[0], me[1], me[2], h] = row_grad[lo : lo + n, 128 * h : 128 * h + 128]

    def ag_axes(k, j):
        axes = [(k + 2 - i) % 3 for i in range(3)]
        return axes[j], {axes[i]: me[axes[i]] for i in range(j + 1, 3)}

    near_block = {}

    def ag_direct(k):
        a, _ = ag_axes(k, 0)
        ref = G_[k].at[me]
        for o in (1, 3, 2):
            _, dev = near(a, o)
            near_block[k, o] = remote(ref, ref, ad_send.at[k, o - 1], ad_recv.at[k, o - 1], dev)

    moves = {}

    def ag_spot(k, j, o, origin, h):
        a, fixed = ag_axes(k, j)
        b, _ = ag_axes(k, j - 1)
        p, _ = near(b, o)
        return G_[k].at[view({**fixed, a: origin, b: p}, h)]

    def ag_open(k, j, o):
        a, _ = ag_axes(k, j)
        for m in range(2):
            for w, (sign, h1) in enumerate(WAYS):
                _, dev = near(a, sign)
                ref = ag_spot(k, j, o, me[a], h1 if m == 0 else 1 - h1)
                moves[k, j, o, w, m] = remote(
                    ref, ref, ag_send.at[k, j - 1, o, w, m], ag_recv.at[k, j - 1, o, w, m], dev
                )

    def ag_pass(k, j, o):
        a, _ = ag_axes(k, j)
        for w, (sign, h1) in enumerate(WAYS):
            _, dev = near(a, sign)
            origin, _ = near(a, 4 - sign)
            moves[k, j, o, w, 0].wait_recv()
            ref = ag_spot(k, j, o, origin, h1)
            moves[k, j, o, w, 2] = remote(
                ref, ref, ag_send.at[k, j - 1, o, w, 2], ag_recv.at[k, j - 1, o, w, 2], dev
            )

    def ag_wait(k, j, m):
        for o in range(4):
            for w in range(2):
                moves[k, j, o, w, m].wait_recv()

    WR = (wra, wrb, wrc)
    WS_AXES = (2, 0, 1)
    WA_AXES = (1, 0, 2)

    def wview(fixed):
        return tuple(fixed.get(a, slice(None)) for a in range(3))

    def ws_open(j):
        a = WS_AXES[j]
        fixed = {WS_AXES[i]: me[WS_AXES[i]] for i in range(j)}
        out = []
        for o in (1, 3, 2):
            c, dev = near(a, o)
            out.append(
                remote(wp.at[wview({**fixed, a: c})], WR[j].at[o - 1], ws_send.at[j, o - 1], ws_recv.at[j, o - 1], dev)
            )
        return out

    def ws_close(j, opened):
        for c in opened:
            c.wait_recv()
        where = wview({WS_AXES[i]: me[WS_AXES[i]] for i in range(j + 1)})
        total = wp[where].astype(f32)
        for o in range(3):
            total = total + WR[j][o].astype(f32)
        (wp if j < 2 else wg)[where] = total.astype(bf16)

    def wa_open(j):
        a = WA_AXES[j]
        fixed = {WA_AXES[i]: me[WA_AXES[i]] for i in range(j, 3)}
        ref = wg.at[wview(fixed)]
        out = []
        for o in (1, 3, 2):
            _, dev = near(a, o)
            out.append(remote(ref, ref, wa_send.at[j, o - 1], wa_recv.at[j, o - 1], dev))
        return out

    def wa_close(opened):
        for c in opened:
            c.wait_recv()

    for k in range(3):
        ag_direct(k)
    for k in range(3):
        ag_open(k, 1, 0)
    part = lax.dot_general(
        agg[...], pg[:, cols], (((0,), (0,)), ((), ())), preferred_element_type=f32
    ).astype(bf16)
    for h in range(2):
        wp[2 * h : 2 * h + 2] = part[:, 128 * h : 128 * h + 128].reshape(2, 4, 4, 16, 128)
    w = ws_open(0)
    act_ref[...] = actv[:, cols]
    acc[...] = jnp.zeros_like(acc)

    def backward(k, o):
        c, _ = near(k, o)
        n = 16 * ROWS[k][1]
        lhs = AT[k][c]
        for h in range(2):
            rhs = G_[k][view({k: c}, h)].reshape(n, 128)
            acc[:, 128 * h : 128 * h + 128] += jnp.dot(lhs, rhs, preferred_element_type=f32)

    for o in (1, 3):
        for k in range(3):
            near_block[k, o].wait_recv()
            ag_open(k, 1, 4 - o)
    for k in range(3):
        ag_pass(k, 1, 0)
    for k in range(3):
        near_block[k, 2].wait_recv()
        ag_open(k, 1, 2)
        ag_open(k, 2, 0)
    ws_close(0, w)
    w = ws_open(1)
    for o in (1, 3, 2):
        for k in range(3):
            ag_pass(k, 1, o)
    for k in range(3):
        ag_wait(k, 1, 1)
        ag_open(k, 2, 1)
        ag_open(k, 2, 3)
    ws_close(1, w)
    w = ws_open(2)
    for k in range(3):
        ag_wait(k, 1, 2)
        ag_open(k, 2, 2)
    for k in range(3):
        ag_pass(k, 2, 0)
    ws_close(2, w)
    w = wa_open(0)
    for k in range(3):
        backward(k, 0)
    for o in (1, 3):
        for k in range(3):
            ag_pass(k, 2, o)
    wa_close(w)
    w = wa_open(1)
    for k in range(3):
        ag_pass(k, 2, 2)
    wa_close(w)
    w = wa_open(2)
    for k in range(3):
        ag_wait(k, 2, 1)
        backward(k, 1)
        backward(k, 3)
    wa_close(w)
    for h in range(2):
        wsum_ref[:, 128 * h : 128 * h + 128] = wg[2 * h : 2 * h + 2].reshape(512, 128)
    for k in (2, 0, 1):
        ag_wait(k, 2, 2)
        backward(k, 2)
    fgrad_ref[...] = (acc[0:128, :] + acc[128:256, :]).astype(bf16)
    for c in started:
        c.wait_send()


def finish(act_in, wsum_in, fgrad_in, act_ref, wgrad_ref, fgrad_ref):
    act_ref[...] = act_in[...]
    fgrad_ref[...] = fgrad_in[...]
    wgrad_ref[...] = wsum_in[...].astype(jnp.float32) * (1.0 / math.sqrt(8192.0))


def layer(own, feat, weight, bias, cot):
    bf16, f32 = jnp.bfloat16, jnp.float32
    V = pltpu.VMEM
    dma = pltpu.SemaphoreType.DMA
    sizes = [n for _, n in ROWS]
    scratch = [V((4, 4, 4, 128, 256), bf16)]
    scratch += [V((4, 256, 16 * n), bf16) for n in sizes]
    scratch += [V((256, 256), bf16)]
    scratch += [V((4, 4, 4, 2, n, 128), bf16) for n in sizes]
    scratch += [V((4, 4, 4, 2, n, 128), bf16) for n in sizes]
    scratch += [V((2, 3, 4, 4, n, 128), bf16) for n in sizes]
    scratch += [V((2, 3, 4, n, 128), bf16) for n in sizes]
    scratch += [V((3, 2, n, 128), bf16) for n in sizes]
    scratch += [V((128, 512), bf16)] * 3
    scratch += [V((4, 4, 4, 16, 128), bf16)]
    scratch += [V((3, 4, 4, 16, 128), bf16), V((3, 4, 16, 128), bf16), V((3, 16, 128), bf16)]
    scratch += [V((4, 4, 4, 16, 128), bf16), V((256, 256), f32)]
    scratch += [dma((4,)), dma((4,)), dma((4,)), dma((1,)), dma((1,))]
    scratch += [dma((3, 2, 2, 6))] * 2 + [dma((3, 3))] * 4
    scratch += [dma((3, 2, 4, 2, 3))] * 2 + [dma((3, 3))] * 4
    whole = pl.BlockSpec(memory_space=pltpu.VMEM)
    return pl.pallas_call(
        layer_kernel,
        out_shape=[
            jax.ShapeDtypeStruct((128, 256), bf16),
            jax.ShapeDtypeStruct((512, 256), bf16),
            jax.ShapeDtypeStruct((128, 256), bf16),
        ],
        in_specs=[pl.BlockSpec(memory_space=pl.ANY)] + [whole] * 4,
        out_specs=[whole] * 3,
        scratch_shapes=scratch,
        compiler_params=pltpu.CompilerParams(collective_id=0, has_side_effects=True),
        name="layer",
    )(own, feat, weight, bias, cot)


def per_device(features, tiles, tile_dest, tile_count, weight, bias, cotangent):
    domains = lax.axis_size("dom")
    own = adjacency(tiles, tile_dest[:, 0], tile_count, domains)
    own = own.reshape(4, 4, 4, 128, 128)
    act, wsum, fgrad = layer(own, features, weight, bias.reshape(1, -1), cotangent)
    whole = pl.BlockSpec(memory_space=pltpu.VMEM)
    return pl.pallas_call(
        finish,
        out_shape=[
            jax.ShapeDtypeStruct(act.shape, act.dtype),
            jax.ShapeDtypeStruct(wsum.shape, jnp.float32),
            jax.ShapeDtypeStruct(fgrad.shape, fgrad.dtype),
        ],
        in_specs=[whole] * 3,
        out_specs=[whole] * 3,
        name="finish",
    )(act, wsum, fgrad)


def solution(mesh):
    in_specs = (
        P("dom", None),
        P(("rep", "dom"), None, None),
        P(("rep", "dom"), None),
        P(("rep", "dom")),
        P(),
        P(),
        P("dom", None),
    )
    out_specs = (P("dom", "rep"), P(None, "rep"), P("dom", "rep"))
    return jax.shard_map(
        per_device, mesh=mesh, in_specs=in_specs, out_specs=out_specs, check_vma=False
    )
```

time: 93.2 us -> 78.8 us (0.85)
  Pallas kernels: 87.4 us -> 78 us
  local copies, waits for them, and re-layouts: 4.81 us -> 0 us
    pallas_call x1, Pallas kernels: 81.6 us -> 71.3 us  [layer(): pl.pallas_call(layer_kernel, out_shape=[jax.ShapeDtypeStruct((128, 256),...]
    unnamed x3 -> x0, local copies, waits for them, and re-layouts: 4.81 us -> none
    pallas_call x0 -> x1, Pallas kernels: none -> 1.82 us  [per_device(): pl.pallas_call(finish, out_shape=[jax.ShapeDtypeStruct(act.shape, act.dty...]
    pallas_call x1, Pallas kernels: 5.78 us -> 4.84 us  [adjacency(): pl.pallas_call(build_blocks, out_shape=jax.ShapeDtypeStruct(shape, jnp.bf...]
where the time goes in v3:
time: 78.8 us; the launch traced here: 78.6 us
  Pallas kernels  78 us (99%)
    pallas_call x1, Pallas kernels, layer(): pl.pallas_call(layer_kernel, out_shape=[jax.ShapeDtypeStruct((128, 256),...  71.3 us
    pallas_call x1, Pallas kernels, adjacency(): pl.pallas_call(build_blocks, out_shape=jax.ShapeDtypeStruct(shape, jnp.bf...  4.84 us
    pallas_call x1, Pallas kernels, per_device(): pl.pallas_call(finish, out_shape=[jax.ShapeDtypeStruct(act.shape, act.dty...  1.82 us

profile of v3, /device:TPU:0, one launch (start us, length us, event | category | flops | bytes accessed | tf_op | source)
XLA Modules:
  0.0 78.6 jit_solution(17606469851442502882)
XLA Ops:
  0.6 4.8 %adjacency.1 = bf16[64,128,128]{2,1,0:T(8,128)(2,1)} custom-call(s32[64]{0:T(128)} %bitcast.5, s32[64]{0:T(128)} %count_ref.1, bf16[64,128,128]{2,1,0:T(8,128)(2,1)} %tiles_ref.1), custom_call_target="tpu_custom_call" | custom-call | tf_op jit(solution)/shard_map/adjacency/pallas_call | solution.py:41
  5.5 71.3 %layer.1 = (bf16[128,256]{1,0:T(8,128)(2,1)}, bf16[512,256]{1,0:T(8,128)(2,1)}, bf16[128,256]{1,0:T(8,128)(2,1)}) custom-call(bf16[4,4,4,128,128]{4,3,2,1,0:T(8,128)(2,1)} %bitcast.3, bf16[128,512]{1,0:T(8,128)(2,1)} %feat_ref.1, bf16[512,512]{1,0:T(8,128)(2,1)} %weight_ref.1, f32[1,512]{1,0:T(1,128)} %bitcast.4, bf16[128,512]{1,0:T(8,128)(2,1)} %cot_ref.1), custom_call_target="tpu_custom_call" | custom-call | tf_op jit(solution)/shard_map/layer/pallas_call | solution.py:470
  76.8 1.8 %finish.1 = (bf16[128,256]{1,0:T(8,128)(2,1)}, f32[512,256]{1,0:T(8,128)}, bf16[128,256]{1,0:T(8,128)(2,1)}) custom-call(bf16[128,256]{1,0:T(8,128)(2,1)} %get-tuple-element.6.act_in, bf16[512,256]{1,0:T(8,128)(2,1)} %get-tuple-element.7.wsum_in, bf16[128,256]{1,0:T(8,128)(2,1)} %get-tuple-element.8.fgrad_in), custom_call_target="tpu_custom_call" | custom-call | tf_op jit(solution)/shard_map/finish/pallas_call | solution.py:491

commit v4 on v3

--- a/solution.py
+++ b/solution.py
@@ -8,48 +8,34 @@
 from jax.sharding import PartitionSpec as P
 
 
-def build_blocks(dest_ref, count_ref, tiles_ref, out_ref, which, used):
-    blocks = out_ref.shape[0]
-
-    @pl.loop(0, blocks)
+def index_tiles(dest_ref, count_ref, which_ref, share_ref, used):
+    @pl.loop(0, used.shape[0], unroll=8)
     def _(b):
         used[b] = 0
-        which[2 * b] = 0
-        which[2 * b + 1] = 0
-
-    @pl.loop(0, tiles_ref.shape[0], unroll=8)
+        for k in range(2):
+            which_ref[2 * b + k] = 0
+            share_ref[2 * b + k] = 0
+
+    @pl.loop(0, dest_ref.shape[0], unroll=8)
     def _(t):
         d = dest_ref[t]
         k = used[d]
-        which[2 * d + k] = t
+        which_ref[2 * d + k] = t
+        share_ref[2 * d + k] = jnp.maximum(count_ref[t], 1)
         used[d] = k + 1
 
-    @pl.loop(0, blocks, unroll=4)
-    def _(b):
-        n = used[b]
-        total = jnp.zeros(out_ref.shape[1:], jnp.float32)
-        for k in range(2):
-            t = which[2 * b + k]
-            c = jnp.full((8, 128), jnp.maximum(count_ref[t], 1), jnp.int32).astype(jnp.float32)
-            s = jnp.where(n > k, lax.rsqrt(c), 0.0)[0:1, :]
-            total = total + tiles_ref[t].astype(jnp.float32) * s
-        out_ref[b] = total.astype(out_ref.dtype)
-
-
-def adjacency(tiles, dest, count, domains):
-    shape = (domains,) + tiles.shape[1:]
+
+def tile_index(dest, count, domains):
+    smem = pl.BlockSpec(memory_space=pltpu.SMEM)
+    shape = jax.ShapeDtypeStruct((2 * domains,), jnp.int32)
     return pl.pallas_call(
-        build_blocks,
-        out_shape=jax.ShapeDtypeStruct(shape, jnp.bfloat16),
-        in_specs=[
-            pl.BlockSpec(memory_space=pltpu.SMEM),
-            pl.BlockSpec(memory_space=pltpu.SMEM),
-            pl.BlockSpec(memory_space=pltpu.VMEM),
-        ],
-        out_specs=pl.BlockSpec(memory_space=pltpu.VMEM),
-        scratch_shapes=[pltpu.SMEM((2 * domains,), jnp.int32), pltpu.SMEM((domains,), jnp.int32)],
-        name="adjacency",
-    )(dest, count, tiles)
+        index_tiles,
+        out_shape=[shape, shape],
+        in_specs=[smem, smem],
+        out_specs=[smem, smem],
+        scratch_shapes=[pltpu.SMEM((domains,), jnp.int32)],
+        name="tile_index",
+    )(dest, count)
 
 
 ROWS = ((0, 48), (48, 48), (96, 32))
@@ -58,9 +44,9 @@
 
 
 def layer_kernel(
-    own_ref, feat_ref, weight_ref, bias_ref, cot_ref,
+    which_ref, share_ref, tiles_ref, feat_ref, weight_ref, bias_ref, cot_ref,
     act_ref, wsum_ref, fgrad_ref,
-    a2, at0, at1, at2, ff, p0, p1, p2, g0, g1, g2,
+    tv, a2, at0, at1, at2, ff, p0, p1, p2, g0, g1, g2,
     ra0, ra1, ra2, rb0, rb1, rb2, rc0, rc1, rc2,
     agg, pg, actv, wp, wra, wrb, wrc, wg, acc,
     own_sem, swap_send, swap_recv, agg_send, agg_recv,
@@ -87,6 +73,27 @@
     for a in range(3):
         for o in (1, 2, 3):
             pl.semaphore_signal(barrier, inc=1, device_id=near(a, o)[1], device_id_type=MESH)
+    load = pltpu.make_async_copy(tiles_ref, tv, own_sem.at[0])
+    load.start()
+    half = 256
+    cols = pl.ds(pl.multiple_of(r * half, half), half)
+    ff[0:128, :] = feat_ref[:, cols]
+    ff[128:256, :] = feat_ref[:, cols]
+    load.wait()
+
+    def build(y, _):
+        for x in range(4):
+            b = 4 * y + x
+            total = jnp.zeros((128, 128), f32)
+            for k in range(2):
+                t = which_ref[2 * b + k]
+                c = jnp.full((8, 128), share_ref[2 * b + k], jnp.int32).astype(f32)
+                scale = jnp.where(c > 0.0, lax.rsqrt(jnp.maximum(c, 1.0)), 0.0)[0:1, :]
+                total = total + tv[t].astype(f32) * scale
+            a2[y // 4, y % 4, x, :, 0:128] = total.astype(bf16)
+        return 0
+
+    lax.fori_loop(0, 16, build, 0)
     pl.semaphore_wait(barrier, 10)
 
     def remote(src, dst, ssem, rsem, dev):
@@ -98,21 +105,17 @@
         started.append(c)
         return c
 
-    half = 256
-    cols = pl.ds(pl.multiple_of(r * half, half), half)
     ORDER = (2, 1, 3, 0)
     WAYS = ((1, 0), (3, 1))
-    swaps, locals_ = [], []
+    swaps = []
     for s, o in enumerate(ORDER):
         i, _ = near(0, o)
         swaps.append(
-            remote(own_ref.at[i], a2.at[i, :, :, :, 128:256], swap_send.at[s], swap_recv.at[s], (other, d))
+            remote(
+                a2.at[i, :, :, :, 0:128], a2.at[i, :, :, :, 128:256],
+                swap_send.at[s], swap_recv.at[s], (other, d),
+            )
         )
-        c = pltpu.make_async_copy(own_ref.at[i], a2.at[i, :, :, :, 0:128], own_sem.at[s])
-        c.start()
-        locals_.append(c)
-    ff[0:128, :] = feat_ref[:, cols]
-    ff[128:256, :] = feat_ref[:, cols]
 
     def view(fixed, h):
         return tuple(fixed.get(a, slice(None)) for a in range(3)) + ((h,) if h is not None else ())
@@ -153,7 +156,6 @@
     lag = None
     for s, o in enumerate(ORDER):
         i, _ = near(0, o)
-        locals_[s].wait()
         swaps[s].wait_recv()
 
         def forward(j, _, i=i):
@@ -446,12 +448,12 @@
     wgrad_ref[...] = wsum_in[...].astype(jnp.float32) * (1.0 / math.sqrt(8192.0))
 
 
-def layer(own, feat, weight, bias, cot):
+def layer(which, share, tiles, feat, weight, bias, cot):
     bf16, f32 = jnp.bfloat16, jnp.float32
     V = pltpu.VMEM
     dma = pltpu.SemaphoreType.DMA
     sizes = [n for _, n in ROWS]
-    scratch = [V((4, 4, 4, 128, 256), bf16)]
+    scratch = [V(tiles.shape, bf16), V((4, 4, 4, 128, 256), bf16)]
     scratch += [V((4, 256, 16 * n), bf16) for n in sizes]
     scratch += [V((256, 256), bf16)]
     scratch += [V((4, 4, 4, 2, n, 128), bf16) for n in sizes]
@@ -463,7 +465,7 @@
     scratch += [V((4, 4, 4, 16, 128), bf16)]
     scratch += [V((3, 4, 4, 16, 128), bf16), V((3, 4, 16, 128), bf16), V((3, 16, 128), bf16)]
     scratch += [V((4, 4, 4, 16, 128), bf16), V((256, 256), f32)]
-    scratch += [dma((4,)), dma((4,)), dma((4,)), dma((1,)), dma((1,))]
+    scratch += [dma((1,)), dma((4,)), dma((4,)), dma((1,)), dma((1,))]
     scratch += [dma((3, 2, 2, 6))] * 2 + [dma((3, 3))] * 4
     scratch += [dma((3, 2, 4, 2, 3))] * 2 + [dma((3, 3))] * 4
     whole = pl.BlockSpec(memory_space=pltpu.VMEM)
@@ -474,19 +476,18 @@
             jax.ShapeDtypeStruct((512, 256), bf16),
             jax.ShapeDtypeStruct((128, 256), bf16),
         ],
-        in_specs=[pl.BlockSpec(memory_space=pl.ANY)] + [whole] * 4,
+        in_specs=[pl.BlockSpec(memory_space=pltpu.SMEM)] * 2 + [pl.BlockSpec(memory_space=pl.ANY)] + [whole] * 4,
         out_specs=[whole] * 3,
         scratch_shapes=scratch,
         compiler_params=pltpu.CompilerParams(collective_id=0, has_side_effects=True),
         name="layer",
-    )(own, feat, weight, bias, cot)
+    )(which, share, tiles, feat, weight, bias, cot)
 
 
 def per_device(features, tiles, tile_dest, tile_count, weight, bias, cotangent):
     domains = lax.axis_size("dom")
-    own = adjacency(tiles, tile_dest[:, 0], tile_count, domains)
-    own = own.reshape(4, 4, 4, 128, 128)
-    act, wsum, fgrad = layer(own, features, weight, bias.reshape(1, -1), cotangent)
+    which, share = tile_index(tile_dest[:, 0], tile_count, domains)
+    act, wsum, fgrad = layer(which, share, tiles, features, weight, bias.reshape(1, -1), cotangent)
     whole = pl.BlockSpec(memory_space=pltpu.VMEM)
     return pl.pallas_call(
         finish,

time: 78.8 us -> 76.8 us (0.975)
  Pallas kernels: 78 us -> 76 us
    pallas_call x1, Pallas kernels: 4.84 us -> 1.81 us  [tile_index(): pl.pallas_call(index_tiles, out_shape=[shape, shape], in_specs=[smem, sme...]
    pallas_call x1, Pallas kernels: 71.3 us -> 72.4 us  [layer(): pl.pallas_call(layer_kernel, out_shape=[jax.ShapeDtypeStruct((128, 256),...]
where the time goes in v4:
time: 76.8 us; the launch traced here: 76.6 us
  Pallas kernels  76 us (99%)
    pallas_call x1, Pallas kernels, layer(): pl.pallas_call(layer_kernel, out_shape=[jax.ShapeDtypeStruct((128, 256),...  72.4 us
    pallas_call x1, Pallas kernels, per_device(): pl.pallas_call(finish, out_shape=[jax.ShapeDtypeStruct(act.shape, act.dty...  1.82 us
    pallas_call x1, Pallas kernels, tile_index(): pl.pallas_call(index_tiles, out_shape=[shape, shape], in_specs=[smem, sme...  1.81 us

profile of v4, /device:TPU:0, one launch (start us, length us, event | category | flops | bytes accessed | tf_op | source)
XLA Modules:
  0.0 76.6 jit_solution(2811572248832899907)
XLA Ops:
  0.6 1.8 %tile_index.1 = (s32[128]{0:T(128)}, s32[128]{0:T(128)}) custom-call(s32[64]{0:T(128)} %bitcast.3, s32[64]{0:T(128)} %count_ref.1), custom_call_target="tpu_custom_call" | custom-call | tf_op jit(solution)/shard_map/tile_index/pallas_call | solution.py:31
  2.4 72.4 %layer.1 = (bf16[128,256]{1,0:T(8,128)(2,1)}, bf16[512,256]{1,0:T(8,128)(2,1)}, bf16[128,256]{1,0:T(8,128)(2,1)}) custom-call(s32[128]{0:T(128)} %get-tuple-element.8.which_ref, s32[128]{0:T(128)} %get-tuple-element.9.share_ref, bf16[64,128,128]{2,1,0:T(8,128)(2,1)} %tiles_ref.1, bf16[128,512]{1,0:T(8,128)(2,1)} %feat_ref.1, bf16[512,512]{1,0:T(8,128)(2,1)} %weight_ref.1, ...), custom_call_target="tpu_custom_call" | custom-call | tf_op jit(solution)/shard_map/layer/pallas_call | solution.py:472
  74.8 1.8 %finish.1 = (bf16[128,256]{1,0:T(8,128)(2,1)}, f32[512,256]{1,0:T(8,128)}, bf16[128,256]{1,0:T(8,128)(2,1)}) custom-call(bf16[128,256]{1,0:T(8,128)(2,1)} %get-tuple-element.10.act_in, bf16[512,256]{1,0:T(8,128)(2,1)} %get-tuple-element.11.wsum_in, bf16[128,256]{1,0:T(8,128)(2,1)} %get-tuple-element.12.fgrad_in), custom_call_target="tpu_custom_call" | custom-call | tf_op jit(solution)/shard_map/finish/pallas_call | solution.py:492

commit v5 on v4

--- a/solution.py
+++ b/solution.py
@@ -38,7 +38,7 @@
     )(dest, count)
 
 
-ROWS = ((0, 48), (48, 48), (96, 32))
+ROWS = ((0, 48), (48, 40), (88, 40))
 STRIDE = (16, 4, 1)
 MESH = pl.DeviceIdType.MESH
 

time: 76.8 us -> 75.2 us (0.979)
  Pallas kernels: 76 us -> 74.3 us
    pallas_call x1, Pallas kernels: 72.4 us -> 70.7 us  [layer(): pl.pallas_call(layer_kernel, out_shape=[jax.ShapeDtypeStruct((128, 256),...]
where the time goes in v5:
time: 75.2 us; the launch traced here: 75 us
  Pallas kernels  74.3 us (99%)
    pallas_call x1, Pallas kernels, layer(): pl.pallas_call(layer_kernel, out_shape=[jax.ShapeDtypeStruct((128, 256),...  70.7 us
    pallas_call x1, Pallas kernels, per_device(): pl.pallas_call(finish, out_shape=[jax.ShapeDtypeStruct(act.shape, act.dty...  1.82 us
    pallas_call x1, Pallas kernels, tile_index(): pl.pallas_call(index_tiles, out_shape=[shape, shape], in_specs=[smem, sme...  1.81 us

profile of v5, /device:TPU:0, one launch (start us, length us, event | category | flops | bytes accessed | tf_op | source)
XLA Modules:
  0.0 75.0 jit_solution(6332009928335236536)
XLA Ops:
  0.6 1.8 %tile_index.1 = (s32[128]{0:T(128)}, s32[128]{0:T(128)}) custom-call(s32[64]{0:T(128)} %bitcast.3, s32[64]{0:T(128)} %count_ref.1), custom_call_target="tpu_custom_call" | custom-call | tf_op jit(solution)/shard_map/tile_index/pallas_call | solution.py:31
  2.4 70.7 %layer.1 = (bf16[128,256]{1,0:T(8,128)(2,1)}, bf16[512,256]{1,0:T(8,128)(2,1)}, bf16[128,256]{1,0:T(8,128)(2,1)}) custom-call(s32[128]{0:T(128)} %get-tuple-element.8.which_ref, s32[128]{0:T(128)} %get-tuple-element.9.share_ref, bf16[64,128,128]{2,1,0:T(8,128)(2,1)} %tiles_ref.1, bf16[128,512]{1,0:T(8,128)(2,1)} %feat_ref.1, bf16[512,512]{1,0:T(8,128)(2,1)} %weight_ref.1, ...), custom_call_target="tpu_custom_call" | custom-call | tf_op jit(solution)/shard_map/layer/pallas_call | solution.py:472
  73.2 1.8 %finish.1 = (bf16[128,256]{1,0:T(8,128)(2,1)}, f32[512,256]{1,0:T(8,128)}, bf16[128,256]{1,0:T(8,128)(2,1)}) custom-call(bf16[128,256]{1,0:T(8,128)(2,1)} %get-tuple-element.10.act_in, bf16[512,256]{1,0:T(8,128)(2,1)} %get-tuple-element.11.wsum_in, bf16[128,256]{1,0:T(8,128)(2,1)} %get-tuple-element.12.fgrad_in), custom_call_target="tpu_custom_call" | custom-call | tf_op jit(solution)/shard_map/finish/pallas_call | solution.py:492
